TPU v7x, 32 devices: a whole 2x2x4 slice. The times are simulated.
32 devices in a mesh: seq: 8 (over z, x), dp: 4 (over y, core).
Axes of the slice: x: 2, y: 2, z: 4, core: 2. Of those that a mesh axis runs over, the one named last changes fastest.
Arguments:
- bases: int32 [4, 16384], P('dp', 'seq'), may hold values from 0 to 3
- stem_table: bfloat16 [60, 256], replicated, may hold values from -1.5 to 1.5
- first_conv_taps: bfloat16 [3, 256, 128], replicated, may hold values from -0.21875 to 0.21875
- first_projection_weight: bfloat16 [128, 256], replicated, may hold values from -0.5 to 0.5
- second_conv_taps: bfloat16 [3, 256, 128], replicated, may hold values from -0.21875 to 0.21875
- second_projection_weight: bfloat16 [128, 256], replicated, may hold values from -0.5 to 0.5
- bin_weight: bfloat16 [1536, 256], P('seq'), may hold values from -0.375 to 0.375
- cotangent: bfloat16 [4, 1536, 128], P('dp', 'seq'), may hold values from -96 to 96
Outputs:
- predictions: bfloat16 [4, 1536, 128], P('dp', 'seq')
- saliency: float32 [4, 4, 16384], P('dp', None, 'seq')
- conv_one_grad: float32 [3, 256, 128], replicated
- proj_one_grad: float32 [128, 256], replicated
- conv_two_grad: float32 [3, 256, 128], replicated
- proj_two_grad: float32 [128, 256], replicated
- bin_weight_grad: float32 [1536, 256], P('seq')
All inputs are finite; a program needn't handle non-finite values.
Results may differ from a plain program's by a relative error of at most 0.015.
Values may be sent and summed in bfloat16 or wider, within the bound.
A program may use at most 64 MiB of HBM per device.

v0:
```python
import jax
import jax.numpy as jnp
from jax import lax
from jax.sharding import PartitionSpec as P

STEM = 15
POOL = 128


def passed_along(value, axis, steps):
    count = lax.axis_size(axis)
    first, last = (max(0, -steps), min(count, count - steps))
    return lax.ppermute(value, axis, [(source, source + steps) for source in range(first, last)])


def with_halo(cells, sides, width):
    for axis, dim in sides:
        count = lax.axis_size(axis)
        ends = count - 1
        head = lax.slice_in_dim(cells, 0, width, axis=dim)
        tail = lax.slice_in_dim(cells, cells.shape[dim] - width, cells.shape[dim], axis=dim)
        cells = jnp.concatenate(
            [
                lax.ppermute(tail, axis, [(i, (i + 1) % count) for i in range(ends)]),
                cells,
                lax.ppermute(head, axis, [((i + 1) % count, i) for i in range(ends)]),
            ],
            axis=dim,
        )
    return cells


def gelu_exact(value):
    return 0.5 * value * (1.0 + jax.scipy.special.erf(value * 0.7071067811865476))


def gelu_slope(value):
    return (
        0.5 * (1.0 + jax.scipy.special.erf(value * 0.7071067811865476))
        + value * jnp.exp(-0.5 * value * value) * 0.3989422804014327
    )


def tap_shift(values, hops):
    return passed_along(values, "seq", hops)


def grad_shift(values, hops):
    return passed_along(values, "seq", hops)


def reduce_grads(conv_raw, proj_raw):
    return lax.psum((conv_raw, proj_raw), ("seq", "dp"))


def residual_block_apply(stream, conv_w, proj_w, hops):
    act = gelu_exact(stream.astype(jnp.float32)).astype(jnp.bfloat16)
    before = tap_shift(act, hops)
    after = tap_shift(act, -hops)
    tap_before = jnp.dot(before, conv_w[0], preferred_element_type=jnp.float32).astype(jnp.bfloat16)
    tap_after = jnp.dot(after, conv_w[2], preferred_element_type=jnp.float32).astype(jnp.bfloat16)
    pre = jnp.dot(act, conv_w[1], preferred_element_type=jnp.float32)
    pre = pre + tap_before.astype(jnp.float32) + tap_after.astype(jnp.float32)
    inner = gelu_exact(pre).astype(jnp.bfloat16)
    result = (
        stream.astype(jnp.float32) + jnp.dot(inner, proj_w, preferred_element_type=jnp.float32)
    ).astype(jnp.bfloat16)
    return (result, (stream, act, before, after, pre, inner))


def residual_block_reverse(incoming, saved, conv_w, proj_w, hops):
    stream, act, before, after, pre, inner = saved
    grad_in = incoming.astype(jnp.bfloat16)
    inner_grad = jnp.dot(grad_in, proj_w.T, preferred_element_type=jnp.float32)
    pre_grad = (inner_grad * gelu_slope(pre)).astype(jnp.bfloat16)
    later = grad_shift(pre_grad, -hops)
    earlier = grad_shift(pre_grad, hops)
    proj_raw = jnp.dot(inner.T, grad_in, preferred_element_type=jnp.float32)
    middle = jnp.dot(act.T, pre_grad, preferred_element_type=jnp.float32)
    conv_raw = jnp.stack(
        [
            jnp.dot(before.T, pre_grad, preferred_element_type=jnp.float32),
            middle,
            jnp.dot(after.T, pre_grad, preferred_element_type=jnp.float32),
        ]
    )
    act_grad = jnp.dot(pre_grad, conv_w[1].T, preferred_element_type=jnp.float32)
    act_grad = act_grad + jnp.dot(later, conv_w[0].T, preferred_element_type=jnp.float32)
    act_grad = act_grad + jnp.dot(earlier, conv_w[2].T, preferred_element_type=jnp.float32)
    outgoing = incoming + act_grad * gelu_slope(stream.astype(jnp.float32))
    conv_sum, proj_sum = reduce_grads(conv_raw, proj_raw)
    return (outgoing, conv_sum, proj_sum)


def per_device(
    bases,
    stem_table,
    first_conv_taps,
    first_projection_weight,
    second_conv_taps,
    second_projection_weight,
    bin_weight,
    cotangent,
):
    length = bases.shape[1]
    width = stem_table.shape[1]
    half = STEM // 2
    bins_dev = length // POOL
    scale = float(lax.axis_size("dp") * lax.axis_size("seq") * length) ** (-0.5)
    padded_ids = with_halo(bases[0] + 1, (("seq", 0),), half)
    taps = jnp.stack([padded_ids[k : k + length] for k in range(STEM)], axis=1)
    letters = jnp.arange(1, 5, dtype=jnp.int32)
    codes = (
        (taps[:, :, None] == letters[None, None, :]).astype(jnp.bfloat16).reshape(length, 4 * STEM)
    )
    stem_pre = jnp.dot(codes, stem_table, preferred_element_type=jnp.float32)
    residual_input_level = gelu_exact(stem_pre).astype(jnp.bfloat16)
    residual_after_first, first_block_stash = residual_block_apply(
        residual_input_level, first_conv_taps, first_projection_weight, 1
    )
    residual_after_second, second_block_stash = residual_block_apply(
        residual_after_first, second_conv_taps, second_projection_weight, 2
    )
    pooled = jnp.mean(
        residual_after_second.astype(jnp.float32).reshape(bins_dev, POOL, width), axis=1
    )
    pooled_act = gelu_exact(pooled).astype(jnp.bfloat16)
    cot_rows = cotangent[0]
    gathered = lax.all_gather(pooled_act, "seq", axis=0, tiled=True)
    preds = lax.dot_general(
        bin_weight, gathered, (((1,), (1,)), ((), ())), preferred_element_type=jnp.float32
    ).astype(jnp.bfloat16)
    bin_part = jnp.dot(cot_rows, gathered, preferred_element_type=jnp.float32)
    summed = lax.psum_scatter(
        lax.dot_general(
            cot_rows, bin_weight, (((0,), (0,)), ((), ())), preferred_element_type=jnp.float32
        ),
        "seq",
        scatter_dimension=0,
        tiled=True,
    )
    bin_total = lax.psum(bin_part, "dp")
    pooled_grad = summed * gelu_slope(pooled)
    gradient_after_second = jnp.repeat(pooled_grad / POOL, POOL, axis=0)
    gradient_after_first, conv_two_sum, proj_two_sum = residual_block_reverse(
        gradient_after_second, second_block_stash, second_conv_taps, second_projection_weight, 2
    )
    gradient_input_level, conv_one_sum, proj_one_sum = residual_block_reverse(
        gradient_after_first, first_block_stash, first_conv_taps, first_projection_weight, 1
    )
    stem_grad = (gradient_input_level * gelu_slope(stem_pre)).astype(jnp.bfloat16)
    code_grad = jnp.dot(stem_grad, stem_table.T, preferred_element_type=jnp.float32)
    padded_grad = with_halo(code_grad.astype(jnp.bfloat16), (("seq", 0),), half).astype(
        code_grad.dtype
    )
    total = jnp.zeros((length, 4), jnp.float32)
    for k in range(STEM):
        start = 2 * half - k
        total = total + padded_grad[start : start + length, 4 * k : 4 * k + 4]
    return (
        preds[None],
        total.T[None],
        conv_one_sum * scale,
        proj_one_sum * scale,
        conv_two_sum * scale,
        proj_two_sum * scale,
        bin_total * scale,
    )


def solution(mesh):
    placed = (P("dp", "seq"), P(), P(), P(), P(), P(), P("seq", None), P("dp", "seq", None))
    return jax.shard_map(
        per_device,
        mesh=mesh,
        in_specs=placed,
        out_specs=(P("dp", "seq", None), P("dp", None, "seq"), P(), P(), P(), P(), P("seq", None)),
        check_vma=False,
    )
```

profile of v0, /device:TPU:0, one launch (start us, length us, event | category | flops | bytes accessed | tf_op | source)
XLA Modules:
  0.0 393.4 jit_solution(10875098786086386174)
XLA Ops:
  7.2 0.7 fusion.105
  8.0 1.3 collective-permute-start.1
  9.3 5.5 %collective-permute-start = (s32[7]{0:T(128)S(1)}, s32[7]{0:T(128)S(1)}, u32[]{:S(2)}, u32[]{:S(2)}) collective-permute-start(s32[7]{0:T(128)S(1)} %get-tuple-element.30), channel_id=1, source_target_pairs={{0,4},{4,8},{8,12},{12,16},{16,20},{20,24},{24,28},{1,5},{5,9},{9,... | collective-permute-start | bytes 92 | tf_op jit(solution)/shard_map/ppermute | solution.py:24
  15.0 1.1 collective-permute-done
  16.2 0.2 stack.84
  16.4 0.1 eq.20
  16.5 0.2 eq.21
  16.7 1.0 fusion.22
  17.8 4.9 %collective-permute-start.2 = (bf16[2048,256]{1,0:T(8,128)(2,1)S(1)}, bf16[2048,256]{1,0:T(8,128)(2,1)S(1)}, u32[]{:S(2)}, u32[]{:S(2)}) collective-permute-start(bf16[2048,256]{1,0:T(8,128)(2,1)S(1)} %get-tuple-element.33), channel_id=1, source_target_pairs={{0,4},{4,8},{8,12},{12,16},{16,20},{20,24},{24,28},{1,5},{5,9},{9,... | collective-permute-start | bytes 3145736 | tf_op jit(solution)/shard_map/ppermute | solution.py:13
  22.7 1.3 collective-permute-start.3
  24.0 0.4 fusion.68
  24.4 41.9 %collective-permute-done.2 = bf16[2048,256]{1,0:T(8,128)(2,1)S(1)} collective-permute-done((bf16[2048,256]{1,0:T(8,128)(2,1)S(1)}, bf16[2048,256]{1,0:T(8,128)(2,1)S(1)}, u32[]{:S(2)}, u32[]{:S(2)}) %collective-permute-start.2) | collective-permute-done | bytes 1048608 | tf_op jit(solution)/shard_map/ppermute | solution.py:13
  66.3 0.4 fusion.16
  66.8 0.4 fusion.14
  67.3 0.5 copy-done.4
  67.8 2.5 fusion.29
  70.4 6.3 %collective-permute-start.4 = (bf16[2048,256]{1,0:T(8,128)(2,1)}, bf16[2048,256]{1,0:T(8,128)(2,1)S(1)}, u32[]{:S(2)}, u32[]{:S(2)}) collective-permute-start(bf16[2048,256]{1,0:T(8,128)(2,1)} %get-tuple-element.35), channel_id=1, source_target_pairs={{0,8},{4,12},{8,16},{12,20},{16,24},{20,28},{1,9},{5,13},{9,17},{1... | collective-permute-start | bytes 3145736 | tf_op jit(solution)/shard_map/ppermute | solution.py:13
  76.6 1.3 collective-permute-start.5
  78.0 0.9 fusion.85
  78.9 1.6 fusion.59
  80.5 19.6 %collective-permute-done.4 = bf16[2048,256]{1,0:T(8,128)(2,1)S(1)} collective-permute-done((bf16[2048,256]{1,0:T(8,128)(2,1)}, bf16[2048,256]{1,0:T(8,128)(2,1)S(1)}, u32[]{:S(2)}, u32[]{:S(2)}) %collective-permute-start.4) | collective-permute-done | bytes 1048608 | tf_op jit(solution)/shard_map/ppermute | solution.py:13
  100.1 0.4 fusion.12
  100.6 3.8 collective-permute-done.5
  104.4 1.4 multiply_convert_fusion.1
  105.8 0.8 copy-done.10
  106.6 0.4 convert_reduce_fusion
  107.0 34.7 %reduce-scatter.2.cloned.1.call-done = f32[16,256]{1,0:T(8,128)} async-done(((f32[128,256]{1,0:T(8,128)}), f32[16,256]{1,0:T(8,128)}) %reduce-scatter.2.cloned.1.call-update) | async-done | bytes 16400 | tf_op jit(solution)/shard_map/reduce_scatter | solution.py:134
  141.7 0.8 multiply_multiply_fusion.3
  142.5 2.0 fusion.107
  144.6 1.4 fusion.7
  146.0 2.5 convolution_bitcast_fusion.2
  148.4 1.5 fusion.57
  149.9 1.3 collective-permute-start.6
  151.2 5.4 %collective-permute-start.7 = (bf16[2048,128]{1,0:T(8,128)(2,1)}, bf16[2048,128]{1,0:T(8,128)(2,1)}, u32[]{:S(2)}, u32[]{:S(2)}) collective-permute-start(bf16[2048,128]{1,0:T(8,128)(2,1)} %fusion.7), channel_id=1, source_target_pairs={{0,8},{4,12},{8,16},{12,20},{16,24},{20,28},{1,9},{5,13},{9,17},{1... | collective-permute-start | bytes 1572872 | tf_op jit(solution)/shard_map/ppermute | solution.py:13
  156.6 33.8 %all_gather.3 = bf16[128,256]{1,0:T(8,128)(2,1)S(1)} all-gather(bf16[16,256]{1,0:T(8,128)(2,1)S(1)} %get-tuple-element.14), channel_id=1, replica_groups=mesh['seq'=8,'dp'=4] {'seq'}, dimensions={0}, use_global_device_ids=true | all-gather | bytes 73728 | tf_op jit(solution)/shard_map/all_gather | solution.py:129
  190.4 0.8 convolution_bitcast_fusion
  191.2 0.8 fusion.35
  192.1 1.9 convolution_bitcast_fusion.1
  194.0 1.8 convolution_bitcast_fusion.3
  195.8 0.8 pad_maximum_fusion.1
  196.6 1.6 convolution_add_fusion.3
  198.2 2.2 bitcast_add_fusion
  200.5 1.1 fusion.47
  201.5 2.0 fusion.8
  203.5 0.5 convolution_bitcast_fusion.5
  204.0 0.5 convolution_bitcast_fusion.4
  204.5 0.2 copy-done.3
  204.7 0.5 convolution_bitcast_fusion.6
  205.2 0.8 pad_maximum_fusion
  206.0 18.0 %all-reduce.4.cloned.1.call-done = f32[192,256]{1,0:T(8,128)} async-done(((f32[192,256]{1,0:T(8,128)}), f32[192,256]{1,0:T(8,128)}) %all-reduce.4.cloned.1.call-update) | async-done | bytes 196624 | tf_op jit(solution)/shard_map/psum | solution.py:142
  224.0 1.6 broadcast_multiply_fusion.2
  225.6 1.3 collective-permute-start.8
  226.9 5.4 %collective-permute-start.9 = (bf16[2048,128]{1,0:T(8,128)(2,1)S(1)}, bf16[2048,128]{1,0:T(8,128)(2,1)}, u32[]{:S(2)}, u32[]{:S(2)}) collective-permute-start(bf16[2048,128]{1,0:T(8,128)(2,1)S(1)} %fusion.8), channel_id=1, source_target_pairs={{0,4},{4,8},{8,12},{12,16},{16,20},{20,24},{24,28},{1,5},{5,9},{9,... | collective-permute-start | bytes 1572872 | tf_op jit(solution)/shard_map/ppermute | solution.py:13
  232.3 1.8 fusion.66
  234.1 132.3 %all-reduce.6.cloned.1.call-done = (f32[3,256,128]{2,1,0:T(8,128)}, f32[128,256]{1,0:T(8,128)}, f32[3,256,128]{2,1,0:T(8,128)}, f32[128,256]{1,0:T(8,128)}) async-done(((f32[3,256,128]{2,1,0:T(8,128)}, f32[128,256]{1,0:T(8,128)}, f32[3,256,128]{2,1,0:T(8,128)}, f32[128,256]{1,0:T(8,128)}), (f32[3,256,128]{2,1,0:T(8,128)}, f32[128,256]{1,0:T(8,128)}, f32[3,256,128]{2,1,0:T(8,128)}, ...) | async-done | bytes 1048592 | tf_op jit(solution)/shard_map/psum | solution.py:53
  366.3 2.0 broadcast_multiply_fusion
  368.4 3.5 convolution_add_fusion.1
  371.9 4.6 %convolution_convert_fusion.4 = bf16[2048,60]{0,1:T(8,128)(2,1)S(1)} fusion(bf16[60,256]{1,0:T(8,128)(2,1)S(1)} %copy-done.28, f32[2048,256]{1,0:T(8,128)S(1)} %bitcast_add_fusion, f32[2048,256]{1,0:T(8,128)} %convolution_add_fusion.1, bf16[2048,128]{1,0:T(8,128)(2,1)} %collective-permute-done.9, f32[2048,256]{1,0:T(8,128)} %copy-done.29, ...), kind=kOutput, calls=%fused_computation.42 | convolution fusion | flops 210362368 | bytes 7159808 | tf_op jit(solution)/shard_map/dot_general | solution.py:152
  376.6 3.4 collective-permute-start.10
  380.0 1.3 collective-permute-start.11
  381.3 0.7 broadcast_multiply_fusion.3
  382.0 3.6 collective-permute-done.11
  385.6 0.3 concatenate.24
  385.9 0.9 fusion.87
  (79 shorter events, 0.9 us)
Async XLA Ops:
  7.2 70.8 %copy-start = (bf16[192,256]{1,0:T(8,128)(2,1)S(1)}, bf16[192,256]{1,0:T(8,128)(2,1)}, u32[]{:S(2)}) copy-start(bf16[192,256]{1,0:T(8,128)(2,1)} %param.14) | copy-start | bytes 294916
  7.2 9.5 %copy-start.27 = (bf16[60,256]{1,0:T(8,128)(2,1)S(1)}, bf16[60,256]{1,0:T(8,128)(2,1)}, u32[]{:S(2)}) copy-start(bf16[60,256]{1,0:T(8,128)(2,1)} %param.9) | copy-start | bytes 92164
  7.2 134.5 %reduce-scatter.2.cloned.1.call-start = ((), (), s32[]{:S(2)}) async-start(), calls=%async_computation.1 | async-start | bytes 147456 | tf_op jit(solution)/shard_map/reduce_scatter | solution.py:134
  8.0 6.9 %collective-permute-start.1 = (s32[7]{0:T(128)S(1)}, s32[7]{0:T(128)S(1)}, u32[]{:S(2)}, u32[]{:S(2)}) collective-permute-start(s32[7]{0:T(128)S(1)} %get-tuple-element.29), channel_id=1, source_target_pairs={{4,0},{8,4},{12,8},{16,12},{20,16},{24,20},{28,24},{5,1},{9,5},{13... | collective-permute-start | bytes 92 | tf_op jit(solution)/shard_map/ppermute | solution.py:26
  9.3 6.8 %collective-permute-start = (s32[7]{0:T(128)S(1)}, s32[7]{0:T(128)S(1)}, u32[]{:S(2)}, u32[]{:S(2)}) collective-permute-start(s32[7]{0:T(128)S(1)} %get-tuple-element.30), channel_id=1, source_target_pairs={{0,4},{4,8},{8,12},{12,16},{16,20},{20,24},{24,28},{1,5},{5,9},{9,... | collective-permute-start | bytes 92 | tf_op jit(solution)/shard_map/ppermute | solution.py:24
  16.7 7.3 %copy-start.15 = (bf16[3,256,128]{2,1,0:T(8,128)(2,1)S(1)}, bf16[3,256,128]{2,1,0:T(8,128)(2,1)}, u32[]{:S(2)}) copy-start(bf16[3,256,128]{2,1,0:T(8,128)(2,1)} %param.10) | copy-start | bytes 589828
  17.7 49.0 %copy-start.8 = (bf16[2048,256]{1,0:T(8,128)(2,1)}, bf16[2048,256]{1,0:T(8,128)(2,1)S(1)}, u32[]{:S(2)}) copy-start(bf16[2048,256]{1,0:T(8,128)(2,1)S(1)} %get-tuple-element.33) | copy-start | bytes 3145732
  17.8 50.0 %copy-start.29 = (f32[2048,256]{1,0:T(8,128)}, f32[2048,256]{1,0:T(8,128)S(1)}, u32[]{:S(2)}) copy-start(f32[2048,256]{1,0:T(8,128)S(1)} %get-tuple-element.34) | copy-start | bytes 6291460
  17.8 48.6 %collective-permute-start.2 = (bf16[2048,256]{1,0:T(8,128)(2,1)S(1)}, bf16[2048,256]{1,0:T(8,128)(2,1)S(1)}, u32[]{:S(2)}, u32[]{:S(2)}) collective-permute-start(bf16[2048,256]{1,0:T(8,128)(2,1)S(1)} %get-tuple-element.33), channel_id=1, source_target_pairs={{0,4},{4,8},{8,12},{12,16},{16,20},{20,24},{24,28},{1,5},{5,9},{9,... | collective-permute-start | bytes 3145736 | tf_op jit(solution)/shard_map/ppermute | solution.py:13
  22.7 44.1 %collective-permute-start.3 = (bf16[2048,256]{1,0:T(8,128)(2,1)S(1)}, bf16[2048,256]{1,0:T(8,128)(2,1)S(1)}, u32[]{:S(2)}, u32[]{:S(2)}) collective-permute-start(bf16[2048,256]{1,0:T(8,128)(2,1)S(1)} %get-tuple-element.33), channel_id=1, source_target_pairs={{4,0},{8,4},{12,8},{16,12},{20,16},{24,20},{28,24},{5,1},{9,5},{13... | collective-permute-start | bytes 3145736 | tf_op jit(solution)/shard_map/ppermute | solution.py:13
  66.3 1.0 copy-start.2
  66.8 1.0 copy-start.23
  66.8 1.0 copy-start.4
  67.8 132.6 %copy-start.1 = (f32[2048,128]{1,0:T(8,128)}, f32[2048,128]{1,0:T(8,128)S(1)}, u32[]{:S(2)}) copy-start(f32[2048,128]{1,0:T(8,128)S(1)} %fusion.14) | copy-start | bytes 3145732
  67.8 10.2 %copy-start.18 = (bf16[1,192,128]{2,1,0:T(8,128)(2,1)S(1)}, bf16[1,192,128]{2,1,0:T(8,128)(2,1)}, u32[]{:S(2)}) copy-start(bf16[1,192,128]{2,1,0:T(8,128)(2,1)} %param.15) | copy-start | bytes 147460
  67.8 11.1 %copy-start.14 = (bf16[3,256,128]{2,1,0:T(8,128)(2,1)S(1)}, bf16[3,256,128]{2,1,0:T(8,128)(2,1)}, u32[]{:S(2)}) copy-start(bf16[3,256,128]{2,1,0:T(8,128)(2,1)} %param.12) | copy-start | bytes 589828
  70.4 29.8 %collective-permute-start.4 = (bf16[2048,256]{1,0:T(8,128)(2,1)}, bf16[2048,256]{1,0:T(8,128)(2,1)S(1)}, u32[]{:S(2)}, u32[]{:S(2)}) collective-permute-start(bf16[2048,256]{1,0:T(8,128)(2,1)} %get-tuple-element.35), channel_id=1, source_target_pairs={{0,8},{4,12},{8,16},{12,20},{16,24},{20,28},{1,9},{5,13},{9,17},{1... | collective-permute-start | bytes 3145736 | tf_op jit(solution)/shard_map/ppermute | solution.py:13
  76.6 27.7 %collective-permute-start.5 = (bf16[2048,256]{1,0:T(8,128)(2,1)}, bf16[2048,256]{1,0:T(8,128)(2,1)S(1)}, u32[]{:S(2)}, u32[]{:S(2)}) collective-permute-start(bf16[2048,256]{1,0:T(8,128)(2,1)} %get-tuple-element.35), channel_id=1, source_target_pairs={{8,0},{12,4},{16,8},{20,12},{24,16},{28,20},{9,1},{13,5},{17,9},{2... | collective-permute-start | bytes 3145736 | tf_op jit(solution)/shard_map/ppermute | solution.py:13
  78.8 145.2 %all-reduce.4.cloned.1.call-start = ((), (), s32[]{:S(2)}) async-start(), calls=%async_computation.2 | async-start | bytes 393216 | tf_op jit(solution)/shard_map/psum | solution.py:142
  100.1 5.6 %copy-start.6 = (bf16[2048,256]{1,0:T(8,128)(2,1)}, bf16[2048,256]{1,0:T(8,128)(2,1)S(1)}, u32[]{:S(2)}) copy-start(bf16[2048,256]{1,0:T(8,128)(2,1)S(1)} %collective-permute-done.4) | copy-start | bytes 3145732
  100.6 6.0 %copy-start.12 = (bf16[2048,256]{1,0:T(8,128)(2,1)S(1)}, bf16[2048,256]{1,0:T(8,128)(2,1)}, u32[]{:S(2)}) copy-start(bf16[2048,256]{1,0:T(8,128)(2,1)} %get-tuple-element.36) | copy-start | bytes 3145732
  100.6 6.0 %copy-start.25 = (bf16[128,256]{1,0:T(8,128)(2,1)S(1)}, bf16[128,256]{1,0:T(8,128)(2,1)}, u32[]{:S(2)}) copy-start(bf16[128,256]{1,0:T(8,128)(2,1)} %param.13) | copy-start | bytes 196612
  104.4 2.6 copy-start.7
  105.8 0.8 copy-start.10
  106.6 38.0 %copy-start.11 = (f32[2048,128]{1,0:T(8,128)S(1)}, f32[2048,128]{1,0:T(8,128)}, u32[]{:S(2)}) copy-start(f32[2048,128]{1,0:T(8,128)} %get-tuple-element.38) | copy-start | bytes 3145732
  141.7 2.9 copy-start.26
  142.4 3.5 copy-start.19
  149.9 46.7 %collective-permute-start.6 = (bf16[2048,128]{1,0:T(8,128)(2,1)}, bf16[2048,128]{1,0:T(8,128)(2,1)}, u32[]{:S(2)}, u32[]{:S(2)}) collective-permute-start(bf16[2048,128]{1,0:T(8,128)(2,1)} %fusion.7), channel_id=1, source_target_pairs={{8,0},{12,4},{16,8},{20,12},{24,16},{28,20},{9,1},{13,5},{17,9},{2... | collective-permute-start | bytes 1572872 | tf_op jit(solution)/shard_map/ppermute | solution.py:13
  151.2 47.0 %collective-permute-start.7 = (bf16[2048,128]{1,0:T(8,128)(2,1)}, bf16[2048,128]{1,0:T(8,128)(2,1)}, u32[]{:S(2)}, u32[]{:S(2)}) collective-permute-start(bf16[2048,128]{1,0:T(8,128)(2,1)} %fusion.7), channel_id=1, source_target_pairs={{0,8},{4,12},{8,16},{12,20},{16,24},{20,28},{1,9},{5,13},{9,17},{1... | collective-permute-start | bytes 1572872 | tf_op jit(solution)/shard_map/ppermute | solution.py:13
  192.0 174.3 %all-reduce.6.cloned.1.call-start = ((), (), s32[]{:S(2)}) async-start(), calls=%async_computation.3 | async-start | bytes 2097152 | tf_op jit(solution)/shard_map/psum | solution.py:53
  192.1 3.7 copy-start.17
  196.6 1.6 copy-start.13
  196.6 1.6 copy-start.20
  200.4 1.1 copy-start.24
  201.5 2.0 copy-start.9
  201.5 2.5 copy-start.5
  203.5 1.2 copy-start.3
  204.7 27.5 %copy-start.16 = (bf16[3,256,128]{2,1,0:T(8,128)(2,1)S(1)}, bf16[3,256,128]{2,1,0:T(8,128)(2,1)}, u32[]{:S(2)}) copy-start(bf16[3,256,128]{2,1,0:T(8,128)(2,1)} %param.10) | copy-start | bytes 589828
  225.6 142.7 %collective-permute-start.8 = (bf16[2048,128]{1,0:T(8,128)(2,1)S(1)}, bf16[2048,128]{1,0:T(8,128)(2,1)}, u32[]{:S(2)}, u32[]{:S(2)}) collective-permute-start(bf16[2048,128]{1,0:T(8,128)(2,1)S(1)} %fusion.8), channel_id=1, source_target_pairs={{4,0},{8,4},{12,8},{16,12},{20,16},{24,20},{28,24},{5,1},{9,5},{13... | collective-permute-start | bytes 1572872 | tf_op jit(solution)/shard_map/ppermute | solution.py:13
  226.9 145.0 %collective-permute-start.9 = (bf16[2048,128]{1,0:T(8,128)(2,1)S(1)}, bf16[2048,128]{1,0:T(8,128)(2,1)}, u32[]{:S(2)}, u32[]{:S(2)}) collective-permute-start(bf16[2048,128]{1,0:T(8,128)(2,1)S(1)} %fusion.8), channel_id=1, source_target_pairs={{0,4},{4,8},{8,12},{12,16},{16,20},{20,24},{24,28},{1,5},{5,9},{9,... | collective-permute-start | bytes 1572872 | tf_op jit(solution)/shard_map/ppermute | solution.py:13
  368.3 3.6 copy-start.28
  371.9 9.4 %copy-start.21 = (f32[128,256]{1,0:T(8,128)S(1)}, f32[128,256]{1,0:T(8,128)}, u32[]{:S(2)}) copy-start(f32[128,256]{1,0:T(8,128)} %get-tuple-element.8) | copy-start | bytes 393220
  371.9 9.4 %copy-start.22 = (f32[128,256]{1,0:T(8,128)S(1)}, f32[128,256]{1,0:T(8,128)}, u32[]{:S(2)}) copy-start(f32[128,256]{1,0:T(8,128)} %get-tuple-element.10) | copy-start | bytes 393220
  376.6 5.4 %collective-permute-start.10 = (bf16[7,60]{0,1:T(8,128)(2,1)S(1)}, bf16[7,60]{0,1:T(8,128)(2,1)S(1)}, u32[]{:S(2)}, u32[]{:S(2)}) collective-permute-start(bf16[7,60]{0,1:T(8,128)(2,1)S(1)} %get-tuple-element.12), channel_id=1, source_target_pairs={{0,4},{4,8},{8,12},{12,16},{16,20},{20,24},{24,28},{1,5},{5,9},{9,... | collective-permute-start | bytes 2528 | tf_op jit(solution)/shard_map/ppermute | solution.py:24
  380.0 5.6 %collective-permute-start.11 = (bf16[7,60]{0,1:T(8,128)(2,1)S(1)}, bf16[7,60]{0,1:T(8,128)(2,1)S(1)}, u32[]{:S(2)}, u32[]{:S(2)}) collective-permute-start(bf16[7,60]{0,1:T(8,128)(2,1)S(1)} %get-tuple-element.11), channel_id=1, source_target_pairs={{4,0},{8,4},{12,8},{16,12},{20,16},{24,20},{28,24},{5,1},{9,5},{13... | collective-permute-start | bytes 2528 | tf_op jit(solution)/shard_map/ppermute | solution.py:26
Sparse Core Ops, SparseCore 0:
  79.0 62.6 reduce-scatter.1
  192.2 31.8 all-reduce.3
  231.1 135.1 all-reduce.5
where the time goes:
time: 394 us; the launch traced here: 393 us
  waiting for transfers between devices  255 us (65%)
  matrix products  40.4 us (10%)
  starting transfers between devices  38.6 us (10%)
  blocking collectives  33.8 us (9%)
  between operations  14.3 us (4%)
  other arithmetic  8.53 us (2%)
    psum x1, waiting for transfers between devices, reduce_grads(): return lax.psum((conv_raw, proj_raw), ('seq', 'dp'))  132 us
    ppermute x8, waiting for transfers between devices, passed_along(): lax.ppermute(value, axis, [(source, source + steps) for source in range(f...  65.3 us
    reduce_scatter x1, waiting for transfers between devices, per_device(): lax.psum_scatter(lax.dot_general(cot_rows, bin_weight, (((0,), (0,)), (()...  34.7 us
    all_gather x1, blocking collectives, per_device(): gathered = lax.all_gather(pooled_act, 'seq', axis=0, tiled=True)  33.8 us
    ppermute x8, starting transfers between devices, passed_along(): lax.ppermute(value, axis, [(source, source + steps) for source in range(f...  27 us
    psum x1, waiting for transfers between devices, per_device(): bin_total = lax.psum(bin_part, 'dp')  18 us
    ppermute x2, starting transfers between devices, with_halo(): lax.ppermute(tail, axis, [(i, (i + 1) % count) for i in range(ends)])  8.85 us
  transfers between devices with their start and end apart: 15, of which 8 were waited for; matrix products, arithmetic and copies ran while one was open for 8% of the time, Pallas kernels for 0%

commit v1 on v0

--- a/solution.py
+++ b/solution.py
@@ -50,7 +50,8 @@
 
 
 def reduce_grads(conv_raw, proj_raw):
-    return lax.psum((conv_raw, proj_raw), ("seq", "dp"))
+    widths_compute = lambda state: jax.lax.psum(jax.lax.psum(state, "dp"), "seq")
+    return widths_compute((conv_raw, proj_raw))
 
 
 def residual_block_apply(stream, conv_w, proj_w, hops):

time: 394 us -> 332 us (0.84)
  waiting for transfers between devices: 255 us -> 208 us
  matrix products: 40.4 us -> 26.3 us
    psum x2, waiting for transfers between devices: 150 us -> 102 us  [the longest x1 67.3 us: reduce_grads(): jax.lax.psum(jax.lax.psum(state, 'dp'), 'seq')]
  transfers between devices with their start and end apart: 15 -> 15, of which waited for: 8 -> 9; matrix products, arithmetic and copies ran while one was open for 8% -> 6% of each run, Pallas kernels for 0% -> 0%
where the time goes in v1:
time: 332 us; the launch traced here: 331 us
  waiting for transfers between devices  208 us (63%)
  starting transfers between devices  37.9 us (11%)
  blocking collectives  31.9 us (10%)
  matrix products  26.3 us (8%)
  between operations  14.3 us (4%)
  other arithmetic  8.66 us (3%)
  local copies, waits for them, and re-layouts  3.91 us (1%)
    ppermute x8, waiting for transfers between devices, passed_along(): lax.ppermute(value, axis, [(source, source + steps) for source in range(f...  67.4 us
    psum x1, waiting for transfers between devices, reduce_grads(): jax.lax.psum(jax.lax.psum(state, 'dp'), 'seq')  67.3 us
    psum x1, waiting for transfers between devices, reduce_grads(): jax.lax.psum(state, 'dp')  34.2 us
    reduce_scatter x1, waiting for transfers between devices, per_device(): lax.psum_scatter(lax.dot_general(cot_rows, bin_weight, (((0,), (0,)), (()...  34.2 us
    all_gather x1, blocking collectives, per_device(): gathered = lax.all_gather(pooled_act, 'seq', axis=0, tiled=True)  31.9 us
    ppermute x8, starting transfers between devices, passed_along(): lax.ppermute(value, axis, [(source, source + steps) for source in range(f...  26.3 us
    ppermute x2, starting transfers between devices, with_halo(): lax.ppermute(tail, axis, [(i, (i + 1) % count) for i in range(ends)])  8.96 us
  transfers between devices with their start and end apart: 15, of which 9 were waited for; matrix products, arithmetic and copies ran while one was open for 6% of the time, Pallas kernels for 0%

profile of v1, /device:TPU:0, one launch (start us, length us, event | category | flops | bytes accessed | tf_op | source)
XLA Modules:
  0.0 331.0 jit_solution(8971818017138685575)
XLA Ops:
  7.2 0.7 fusion.105
  8.0 1.3 collective-permute-start.1
  9.3 5.5 %collective-permute-start = (s32[7]{0:T(128)S(1)}, s32[7]{0:T(128)S(1)}, u32[]{:S(2)}, u32[]{:S(2)}) collective-permute-start(s32[7]{0:T(128)S(1)} %get-tuple-element.35), channel_id=1, source_target_pairs={{0,4},{4,8},{8,12},{12,16},{16,20},{20,24},{24,28},{1,5},{5,9},{9,... | collective-permute-start | bytes 92 | tf_op jit(solution)/shard_map/ppermute | solution.py:24
  15.0 1.1 collective-permute-done
  16.2 0.2 stack.84
  16.7 1.0 fusion.22
  17.8 4.9 %collective-permute-start.2 = (bf16[2048,256]{1,0:T(8,128)(2,1)S(1)}, bf16[2048,256]{1,0:T(8,128)(2,1)S(1)}, u32[]{:S(2)}, u32[]{:S(2)}) collective-permute-start(bf16[2048,256]{1,0:T(8,128)(2,1)S(1)} %get-tuple-element.38), channel_id=1, source_target_pairs={{0,4},{4,8},{8,12},{12,16},{16,20},{20,24},{24,28},{1,5},{5,9},{9,... | collective-permute-start | bytes 3145736 | tf_op jit(solution)/shard_map/ppermute | solution.py:13
  22.7 1.3 collective-permute-start.3
  24.0 0.4 fusion.68
  24.4 41.9 %collective-permute-done.2 = bf16[2048,256]{1,0:T(8,128)(2,1)S(1)} collective-permute-done((bf16[2048,256]{1,0:T(8,128)(2,1)S(1)}, bf16[2048,256]{1,0:T(8,128)(2,1)S(1)}, u32[]{:S(2)}, u32[]{:S(2)}) %collective-permute-start.2) | collective-permute-done | bytes 1048608 | tf_op jit(solution)/shard_map/ppermute | solution.py:13
  66.3 0.4 fusion.16
  66.8 0.4 fusion.14
  67.3 0.5 copy-done.5
  67.8 2.3 fusion.29
  70.1 6.3 %collective-permute-start.4 = (bf16[2048,256]{1,0:T(8,128)(2,1)S(1)}, bf16[2048,256]{1,0:T(8,128)(2,1)S(1)}, u32[]{:S(2)}, u32[]{:S(2)}) collective-permute-start(bf16[2048,256]{1,0:T(8,128)(2,1)S(1)} %get-tuple-element.40), channel_id=1, source_target_pairs={{0,8},{4,12},{8,16},{12,20},{16,24},{20,28},{1,9},{5,13},{9,17},{1... | collective-permute-start | bytes 3145736 | tf_op jit(solution)/shard_map/ppermute | solution.py:13
  76.4 1.3 collective-permute-start.5
  77.7 0.9 fusion.85
  78.6 0.4 fusion.59
  79.0 20.5 %collective-permute-done.4 = bf16[2048,256]{1,0:T(8,128)(2,1)S(1)} collective-permute-done((bf16[2048,256]{1,0:T(8,128)(2,1)S(1)}, bf16[2048,256]{1,0:T(8,128)(2,1)S(1)}, u32[]{:S(2)}, u32[]{:S(2)}) %collective-permute-start.4) | collective-permute-done | bytes 1048608 | tf_op jit(solution)/shard_map/ppermute | solution.py:13
  99.5 0.4 fusion.12
  100.0 3.9 %collective-permute-done.5 = bf16[2048,256]{1,0:T(8,128)(2,1)S(1)} collective-permute-done((bf16[2048,256]{1,0:T(8,128)(2,1)S(1)}, bf16[2048,256]{1,0:T(8,128)(2,1)S(1)}, u32[]{:S(2)}, u32[]{:S(2)}) %collective-permute-start.5) | collective-permute-done | bytes 1048608 | tf_op jit(solution)/shard_map/ppermute | solution.py:13
  103.9 1.5 multiply_convert_fusion.1
  105.3 0.8 copy-done.9
  106.2 1.0 convert_reduce_fusion
  107.2 34.2 %reduce-scatter.2.cloned.1.call-done = f32[16,256]{1,0:T(8,128)} async-done(((f32[128,256]{1,0:T(8,128)}), f32[16,256]{1,0:T(8,128)}) %reduce-scatter.2.cloned.1.call-update) | async-done | bytes 16400 | tf_op jit(solution)/shard_map/reduce_scatter | solution.py:135
  141.4 0.8 multiply_multiply_fusion.3
  142.3 2.0 fusion.107
  144.4 0.6 fusion.7
  145.0 0.5 convolution_bitcast_fusion.2
  145.4 1.3 collective-permute-start.6
  146.7 4.6 %collective-permute-start.7 = (bf16[2048,128]{1,0:T(8,128)(2,1)S(1)}, bf16[2048,128]{1,0:T(8,128)(2,1)S(1)}, u32[]{:S(2)}, u32[]{:S(2)}) collective-permute-start(bf16[2048,128]{1,0:T(8,128)(2,1)S(1)} %fusion.7), channel_id=1, source_target_pairs={{0,8},{4,12},{8,16},{12,20},{16,24},{20,28},{1,9},{5,13},{9,17},{1... | collective-permute-start | bytes 1572872 | tf_op jit(solution)/shard_map/ppermute | solution.py:13
  151.3 0.5 convolution_bitcast_fusion.1
  151.8 0.5 convolution_bitcast_fusion.3
  152.3 0.8 pad_maximum_fusion.1
  153.1 31.9 %all_gather.3 = bf16[128,256]{1,0:T(8,128)(2,1)S(1)} all-gather(bf16[16,256]{1,0:T(8,128)(2,1)S(1)} %get-tuple-element.19), channel_id=1, replica_groups=mesh['seq'=8,'dp'=4] {'seq'}, dimensions={0}, use_global_device_ids=true | all-gather | bytes 73728 | tf_op jit(solution)/shard_map/all_gather | solution.py:130
  184.9 0.4 fusion.57
  185.4 0.8 convolution_bitcast_fusion
  186.2 0.4 convolution_add_fusion.3
  186.7 0.8 copy-done.12
  187.4 1.1 bitcast_add_fusion
  188.6 0.6 fusion.8
  189.2 0.6 copy-done.8
  189.8 0.5 convolution_bitcast_fusion.5
  190.2 1.3 collective-permute-start.8
  191.6 5.4 %collective-permute-start.9 = (bf16[2048,128]{1,0:T(8,128)(2,1)S(1)}, bf16[2048,128]{1,0:T(8,128)(2,1)}, u32[]{:S(2)}, u32[]{:S(2)}) collective-permute-start(bf16[2048,128]{1,0:T(8,128)(2,1)S(1)} %fusion.8), channel_id=1, source_target_pairs={{0,4},{4,8},{8,12},{12,16},{16,20},{20,24},{24,28},{1,5},{5,9},{9,... | collective-permute-start | bytes 1572872 | tf_op jit(solution)/shard_map/ppermute | solution.py:13
  196.9 0.5 convolution_bitcast_fusion.4
  197.4 0.5 convolution_bitcast_fusion.6
  197.9 0.8 pad_maximum_fusion
  198.7 1.1 fusion.47
  199.8 0.4 fusion.66
  200.3 1.1 collective-permute-done.8
  201.3 1.8 convolution_add_fusion.1
  203.1 34.2 %all-reduce.7.cloned.1.call-done = (f32[3,256,128]{2,1,0:T(8,128)}, f32[128,256]{1,0:T(8,128)}, f32[3,256,128]{2,1,0:T(8,128)}, f32[128,256]{1,0:T(8,128)}, f32[192,256]{1,0:T(8,128)}) async-done(((f32[3,256,128]{2,1,0:T(8,128)}, f32[128,256]{1,0:T(8,128)}, f32[3,256,128]{2,1,0:T(8,128)}, f32[128,256]{1,0:T(8,128)}, f32[192,256]{1,0:T(8,128)}), (f32[3,256,128]{2,1,0:T(8,128)}, f32[128,256]{1,0:T(8,128)}, ...) | async-done | bytes 1245200 | tf_op jit(solution)/shard_map/psum | solution.py:53
  237.4 4.6 %convolution_convert_fusion.4 = bf16[2048,60]{0,1:T(8,128)(2,1)S(1)} fusion(bf16[60,256]{1,0:T(8,128)(2,1)S(1)} %copy-done.22, f32[2048,256]{1,0:T(8,128)S(1)} %bitcast_add_fusion, f32[2048,256]{1,0:T(8,128)} %convolution_add_fusion.1, bf16[2048,128]{1,0:T(8,128)(2,1)} %collective-permute-done.9, f32[2048,256]{1,0:T(8,128)} %copy-done.23, ...), kind=kOutput, calls=%fused_computation.42 | convolution fusion | flops 210362368 | bytes 7159808 | tf_op jit(solution)/shard_map/dot_general | solution.py:153
  242.0 3.5 %collective-permute-start.10 = (bf16[7,60]{0,1:T(8,128)(2,1)S(1)}, bf16[7,60]{0,1:T(8,128)(2,1)S(1)}, u32[]{:S(2)}, u32[]{:S(2)}) collective-permute-start(bf16[7,60]{0,1:T(8,128)(2,1)S(1)} %get-tuple-element.17), channel_id=1, source_target_pairs={{0,4},{4,8},{8,12},{12,16},{16,20},{20,24},{24,28},{1,5},{5,9},{9,... | collective-permute-start | bytes 2528 | tf_op jit(solution)/shard_map/ppermute | solution.py:24
  245.5 1.3 collective-permute-start.11
  246.8 0.8 fusion.35
  247.7 3.8 %collective-permute-done.11 = bf16[7,60]{0,1:T(8,128)(2,1)S(1)} collective-permute-done((bf16[7,60]{0,1:T(8,128)(2,1)S(1)}, bf16[7,60]{0,1:T(8,128)(2,1)S(1)}, u32[]{:S(2)}, u32[]{:S(2)}) %collective-permute-start.11) | collective-permute-done | bytes 872 | tf_op jit(solution)/shard_map/ppermute | solution.py:26
  251.5 0.3 concatenate.24
  251.8 0.9 fusion.87
  252.7 0.7 broadcast_multiply_fusion.2
  253.4 67.3 %all-reduce.5.cloned.1.call-done = (f32[3,256,128]{2,1,0:T(8,128)}, f32[128,256]{1,0:T(8,128)}, f32[3,256,128]{2,1,0:T(8,128)}, f32[128,256]{1,0:T(8,128)}) async-done(((f32[3,256,128]{2,1,0:T(8,128)}, f32[128,256]{1,0:T(8,128)}, f32[3,256,128]{2,1,0:T(8,128)}, f32[128,256]{1,0:T(8,128)}), (f32[3,256,128]{2,1,0:T(8,128)}, f32[128,256]{1,0:T(8,128)}, f32[3,256,128]{2,1,0:T(8,128)}, ...) | async-done | bytes 1048592 | tf_op jit(solution)/shard_map/psum | solution.py:53
  320.7 1.7 broadcast_multiply_fusion.3
  322.4 2.0 broadcast_multiply_fusion
  (67 shorter events, 1.2 us)
Async XLA Ops:
  7.2 70.5 %copy-start = (bf16[192,256]{1,0:T(8,128)(2,1)S(1)}, bf16[192,256]{1,0:T(8,128)(2,1)}, u32[]{:S(2)}) copy-start(bf16[192,256]{1,0:T(8,128)(2,1)} %param.14) | copy-start | bytes 294916
  7.2 9.5 %copy-start.21 = (bf16[60,256]{1,0:T(8,128)(2,1)S(1)}, bf16[60,256]{1,0:T(8,128)(2,1)}, u32[]{:S(2)}) copy-start(bf16[60,256]{1,0:T(8,128)(2,1)} %param.9) | copy-start | bytes 92164
  7.2 134.2 %reduce-scatter.2.cloned.1.call-start = ((), (), s32[]{:S(2)}) async-start(), calls=%async_computation.1 | async-start | bytes 147456 | tf_op jit(solution)/shard_map/reduce_scatter | solution.py:135
  8.0 6.9 %collective-permute-start.1 = (s32[7]{0:T(128)S(1)}, s32[7]{0:T(128)S(1)}, u32[]{:S(2)}, u32[]{:S(2)}) collective-permute-start(s32[7]{0:T(128)S(1)} %get-tuple-element.34), channel_id=1, source_target_pairs={{4,0},{8,4},{12,8},{16,12},{20,16},{24,20},{28,24},{5,1},{9,5},{13... | collective-permute-start | bytes 92 | tf_op jit(solution)/shard_map/ppermute | solution.py:26
  9.3 6.8 %collective-permute-start = (s32[7]{0:T(128)S(1)}, s32[7]{0:T(128)S(1)}, u32[]{:S(2)}, u32[]{:S(2)}) collective-permute-start(s32[7]{0:T(128)S(1)} %get-tuple-element.35), channel_id=1, source_target_pairs={{0,4},{4,8},{8,12},{12,16},{16,20},{20,24},{24,28},{1,5},{5,9},{9,... | collective-permute-start | bytes 92 | tf_op jit(solution)/shard_map/ppermute | solution.py:24
  16.7 7.3 %copy-start.14 = (bf16[3,256,128]{2,1,0:T(8,128)(2,1)S(1)}, bf16[3,256,128]{2,1,0:T(8,128)(2,1)}, u32[]{:S(2)}) copy-start(bf16[3,256,128]{2,1,0:T(8,128)(2,1)} %param.10) | copy-start | bytes 589828
  17.7 49.0 %copy-start.7 = (bf16[2048,256]{1,0:T(8,128)(2,1)}, bf16[2048,256]{1,0:T(8,128)(2,1)S(1)}, u32[]{:S(2)}) copy-start(bf16[2048,256]{1,0:T(8,128)(2,1)S(1)} %get-tuple-element.38) | copy-start | bytes 3145732
  17.8 50.0 %copy-start.23 = (f32[2048,256]{1,0:T(8,128)}, f32[2048,256]{1,0:T(8,128)S(1)}, u32[]{:S(2)}) copy-start(f32[2048,256]{1,0:T(8,128)S(1)} %get-tuple-element.39) | copy-start | bytes 6291460
  17.8 48.6 %collective-permute-start.2 = (bf16[2048,256]{1,0:T(8,128)(2,1)S(1)}, bf16[2048,256]{1,0:T(8,128)(2,1)S(1)}, u32[]{:S(2)}, u32[]{:S(2)}) collective-permute-start(bf16[2048,256]{1,0:T(8,128)(2,1)S(1)} %get-tuple-element.38), channel_id=1, source_target_pairs={{0,4},{4,8},{8,12},{12,16},{16,20},{20,24},{24,28},{1,5},{5,9},{9,... | collective-permute-start | bytes 3145736 | tf_op jit(solution)/shard_map/ppermute | solution.py:13
  22.7 44.1 %collective-permute-start.3 = (bf16[2048,256]{1,0:T(8,128)(2,1)S(1)}, bf16[2048,256]{1,0:T(8,128)(2,1)S(1)}, u32[]{:S(2)}, u32[]{:S(2)}) collective-permute-start(bf16[2048,256]{1,0:T(8,128)(2,1)S(1)} %get-tuple-element.38), channel_id=1, source_target_pairs={{4,0},{8,4},{12,8},{16,12},{20,16},{24,20},{28,24},{5,1},{9,5},{13... | collective-permute-start | bytes 3145736 | tf_op jit(solution)/shard_map/ppermute | solution.py:13
  66.3 1.0 copy-start.3
  66.8 1.0 copy-start.18
  66.8 1.0 copy-start.5
  67.8 2.3 copy-start.1
  67.8 9.9 %copy-start.17 = (bf16[1,192,128]{2,1,0:T(8,128)(2,1)S(1)}, bf16[1,192,128]{2,1,0:T(8,128)(2,1)}, u32[]{:S(2)}) copy-start(bf16[1,192,128]{2,1,0:T(8,128)(2,1)} %param.15) | copy-start | bytes 147460
  67.8 10.8 %copy-start.13 = (bf16[3,256,128]{2,1,0:T(8,128)(2,1)S(1)}, bf16[3,256,128]{2,1,0:T(8,128)(2,1)}, u32[]{:S(2)}) copy-start(bf16[3,256,128]{2,1,0:T(8,128)(2,1)} %param.12) | copy-start | bytes 589828
  70.1 29.4 %collective-permute-start.4 = (bf16[2048,256]{1,0:T(8,128)(2,1)S(1)}, bf16[2048,256]{1,0:T(8,128)(2,1)S(1)}, u32[]{:S(2)}, u32[]{:S(2)}) collective-permute-start(bf16[2048,256]{1,0:T(8,128)(2,1)S(1)} %get-tuple-element.40), channel_id=1, source_target_pairs={{0,8},{4,12},{8,16},{12,20},{16,24},{20,28},{1,9},{5,13},{9,17},{1... | collective-permute-start | bytes 3145736 | tf_op jit(solution)/shard_map/ppermute | solution.py:13
  76.4 27.5 %collective-permute-start.5 = (bf16[2048,256]{1,0:T(8,128)(2,1)S(1)}, bf16[2048,256]{1,0:T(8,128)(2,1)S(1)}, u32[]{:S(2)}, u32[]{:S(2)}) collective-permute-start(bf16[2048,256]{1,0:T(8,128)(2,1)S(1)} %get-tuple-element.40), channel_id=1, source_target_pairs={{8,0},{12,4},{16,8},{20,12},{24,16},{28,20},{9,1},{13,5},{17,9},{2... | collective-permute-start | bytes 3145736 | tf_op jit(solution)/shard_map/ppermute | solution.py:13
  78.6 158.8 %all-reduce.7.cloned.1.call-start = ((), (), s32[]{:S(2)}) async-start(), calls=%async_computation.3 | async-start | bytes 2490368 | tf_op jit(solution)/shard_map/psum | solution.py:53
  100.0 6.2 %copy-start.11 = (bf16[2048,256]{1,0:T(8,128)(2,1)S(1)}, bf16[2048,256]{1,0:T(8,128)(2,1)}, u32[]{:S(2)}) copy-start(bf16[2048,256]{1,0:T(8,128)(2,1)} %get-tuple-element.41) | copy-start | bytes 3145732
  100.0 6.2 %copy-start.19 = (bf16[128,256]{1,0:T(8,128)(2,1)S(1)}, bf16[128,256]{1,0:T(8,128)(2,1)}, u32[]{:S(2)}) copy-start(bf16[128,256]{1,0:T(8,128)(2,1)} %param.13) | copy-start | bytes 196612
  105.3 0.8 copy-start.9
  141.4 3.0 copy-start.10
  141.4 3.0 copy-start.20
  145.4 40.8 %collective-permute-start.6 = (bf16[2048,128]{1,0:T(8,128)(2,1)S(1)}, bf16[2048,128]{1,0:T(8,128)(2,1)S(1)}, u32[]{:S(2)}, u32[]{:S(2)}) collective-permute-start(bf16[2048,128]{1,0:T(8,128)(2,1)S(1)} %fusion.7), channel_id=1, source_target_pairs={{8,0},{12,4},{16,8},{20,12},{24,16},{28,20},{9,1},{13,5},{17,9},{2... | collective-permute-start | bytes 1572872 | tf_op jit(solution)/shard_map/ppermute | solution.py:13
  146.7 39.9 %collective-permute-start.7 = (bf16[2048,128]{1,0:T(8,128)(2,1)S(1)}, bf16[2048,128]{1,0:T(8,128)(2,1)S(1)}, u32[]{:S(2)}, u32[]{:S(2)}) collective-permute-start(bf16[2048,128]{1,0:T(8,128)(2,1)S(1)} %fusion.7), channel_id=1, source_target_pairs={{0,8},{4,12},{8,16},{12,20},{16,24},{20,28},{1,9},{5,13},{9,17},{1... | collective-permute-start | bytes 1572872 | tf_op jit(solution)/shard_map/ppermute | solution.py:13
  186.2 1.2 copy-start.12
  186.6 1.9 copy-start.2
  188.5 1.2 copy-start.8
  188.6 8.4 %copy-start.6 = (bf16[2048,256]{1,0:T(8,128)(2,1)S(1)}, bf16[2048,256]{1,0:T(8,128)(2,1)}, u32[]{:S(2)}) copy-start(bf16[2048,256]{1,0:T(8,128)(2,1)} %copy-done.5) | copy-start | bytes 3145732
  189.8 7.6 %copy-start.4 = (bf16[2048,256]{1,0:T(8,128)(2,1)S(1)}, bf16[2048,256]{1,0:T(8,128)(2,1)}, u32[]{:S(2)}) copy-start(bf16[2048,256]{1,0:T(8,128)(2,1)} %copy-done.3) | copy-start | bytes 3145732
  190.2 11.1 %collective-permute-start.8 = (bf16[2048,128]{1,0:T(8,128)(2,1)S(1)}, bf16[2048,128]{1,0:T(8,128)(2,1)S(1)}, u32[]{:S(2)}, u32[]{:S(2)}) collective-permute-start(bf16[2048,128]{1,0:T(8,128)(2,1)S(1)} %fusion.8), channel_id=1, source_target_pairs={{4,0},{8,4},{12,8},{16,12},{20,16},{24,20},{28,24},{5,1},{9,5},{13... | collective-permute-start | bytes 1572872 | tf_op jit(solution)/shard_map/ppermute | solution.py:13
  191.6 45.8 %collective-permute-start.9 = (bf16[2048,128]{1,0:T(8,128)(2,1)S(1)}, bf16[2048,128]{1,0:T(8,128)(2,1)}, u32[]{:S(2)}, u32[]{:S(2)}) collective-permute-start(bf16[2048,128]{1,0:T(8,128)(2,1)S(1)} %fusion.8), channel_id=1, source_target_pairs={{0,4},{4,8},{8,12},{12,16},{16,20},{20,24},{24,28},{1,5},{5,9},{9,... | collective-permute-start | bytes 1572872 | tf_op jit(solution)/shard_map/ppermute | solution.py:13
  198.7 1.1 copy-start.15
  199.8 120.9 %all-reduce.5.cloned.1.call-start = ((), (), s32[]{:S(2)}) async-start(), calls=%async_computation.2 | async-start | bytes 2097152 | tf_op jit(solution)/shard_map/psum | solution.py:53
  200.3 37.1 %copy-start.22 = (bf16[60,256]{1,0:T(8,128)(2,1)S(1)}, bf16[60,256]{1,0:T(8,128)(2,1)}, u32[]{:S(2)}) copy-start(bf16[60,256]{1,0:T(8,128)(2,1)} %param.9) | copy-start | bytes 92164
  242.0 10.8 %copy-start.16 = (f32[192,256]{1,0:T(8,128)S(1)}, f32[192,256]{1,0:T(8,128)}, u32[]{:S(2)}) copy-start(f32[192,256]{1,0:T(8,128)} %get-tuple-element.15) | copy-start | bytes 589828
  242.0 5.6 %collective-permute-start.10 = (bf16[7,60]{0,1:T(8,128)(2,1)S(1)}, bf16[7,60]{0,1:T(8,128)(2,1)S(1)}, u32[]{:S(2)}, u32[]{:S(2)}) collective-permute-start(bf16[7,60]{0,1:T(8,128)(2,1)S(1)} %get-tuple-element.17), channel_id=1, source_target_pairs={{0,4},{4,8},{8,12},{12,16},{16,20},{20,24},{24,28},{1,5},{5,9},{9,... | collective-permute-start | bytes 2528 | tf_op jit(solution)/shard_map/ppermute | solution.py:24
  245.5 5.9 %collective-permute-start.11 = (bf16[7,60]{0,1:T(8,128)(2,1)S(1)}, bf16[7,60]{0,1:T(8,128)(2,1)S(1)}, u32[]{:S(2)}, u32[]{:S(2)}) collective-permute-start(bf16[7,60]{0,1:T(8,128)(2,1)S(1)} %get-tuple-element.16), channel_id=1, source_target_pairs={{4,0},{8,4},{12,8},{16,12},{20,16},{24,20},{28,24},{5,1},{9,5},{13... | collective-permute-start | bytes 2528 | tf_op jit(solution)/shard_map/ppermute | solution.py:26
Sparse Core Ops, SparseCore 0:
  78.7 62.6 reduce-scatter.1
  199.9 37.3 all-reduce.6
  241.6 79.0 all-reduce.4
